TPU v7x, 256 devices: a whole 4x4x8 slice. The times are simulated.
256 devices in a mesh: wide: 32 (over x, z), narrow: 8 (over y, core).
Axes of the slice: x: 4, y: 4, z: 8, core: 2. Of those that a mesh axis runs over, the one named last changes fastest.
Arguments:
- hidden_in: bfloat16 [16384, 1664], P(('wide', 'narrow')), may hold values from -3 to 3
- queries: bfloat16 [16, 1024, 1664], P('narrow', 'wide'), may hold values from -24 to 24
- keys: bfloat16 [16, 1024, 1664], P('narrow', 'wide'), may hold values from -24 to 24
- values: bfloat16 [16, 1024, 1664], P('narrow', 'wide'), may hold values from -12 to 12
- out_weight: bfloat16 [1664, 1664], P('narrow', 'wide'), may hold values from -0.25 to 0.25
- merge_weight: bfloat16 [4, 1664, 1664], P(None, 'narrow', 'wide'), may hold values from -0.125 to 0.125
- segment_ids: int32 [4096], P('wide'), may hold values from 0 to 15, never falling along the last dimension, each value on 1 to 2560 neighbouring positions
- owners: int32 [4096, 1], P('wide'), may hold values from 0 to 31; in each aligned block of 128 rows (0 to 127, 128 to 255, ...) at most 8 rows name the same one
Outputs:
- hidden_out: bfloat16 [16384, 1664], P(('wide', 'narrow'))
- delivered: bfloat16 [8192, 1664], P('wide', 'narrow')
Inputs may be any that keep to these rules, and one draw needn't show every extreme that they name: `segment_ids`: never falling along the tokens; the largest image or clip holds exactly 2560 merged tokens. `owners`: among the merged tokens of one index of wide, at most 8 share an owner, and exactly 8 do for some owner.
All inputs are finite; a program needn't handle non-finite values.
Results may differ from a plain program's by a relative error of at most 0.025.
Values may be sent and summed in bfloat16 or wider, within the bound.
A program may use at most 64 MiB of HBM per device.

v0:
```python
import math
import jax
import jax.numpy as jnp
from jax import lax
from jax.sharding import PartitionSpec as P

HEAD_DIM = 104
NEG = -1e30


def shards(hidden_in, queries, keys, values, out_weight, merge_weight, segment_ids, owners):
    heads_here, packed_rows, packed_width = queries.shape
    tok_rows = packed_rows * 16
    local_width = heads_here * HEAD_DIM
    scale = 1.0 / math.sqrt(HEAD_DIM)
    tok_seg = jnp.repeat(segment_ids, 4)
    seg_packed = tok_seg.reshape(1, packed_rows, 16)
    gathered_out, gathered_merge = (
        lax.all_gather(out_weight, "wide", axis=1, tiled=True),
        lax.all_gather(merge_weight, "wide", axis=2, tiled=True),
    )
    query_heads = queries.reshape(heads_here, tok_rows, HEAD_DIM)

    def key_block(carry, key_rows, value_rows, seg_rows):
        keep = tok_seg[:, None] == seg_rows[None, :]
        best, total, accum = carry
        key_heads = key_rows.reshape(heads_here, -1, HEAD_DIM)
        value_heads = value_rows.reshape(heads_here, -1, HEAD_DIM)
        scores = (
            jnp.einsum("hqd,hkd->hqk", query_heads, key_heads, preferred_element_type=jnp.float32)
            * scale
        )
        scores = jnp.where(keep[None], scores, NEG)
        new_best = jnp.maximum(best, jnp.max(scores, axis=-1))
        weights = jnp.where(keep[None], jnp.exp(scores - new_best[..., None]), 0.0)
        factor = jnp.exp(best - new_best)
        total = total * factor + jnp.sum(weights, axis=-1)
        accum = accum * factor[..., None] + jnp.einsum(
            "hqk,hkd->hqd",
            weights.astype(jnp.bfloat16),
            value_heads,
            preferred_element_type=jnp.float32,
        )
        return (new_best, total, accum)

    start_state = (
        jnp.full((heads_here, tok_rows), NEG, jnp.float32),
        jnp.zeros((heads_here, tok_rows), jnp.float32),
        jnp.zeros((heads_here, tok_rows, HEAD_DIM), jnp.float32),
    )
    carry = start_state
    key_rows = lax.all_gather(keys, "wide", axis=1, tiled=True)
    value_rows = lax.all_gather(values, "wide", axis=1, tiled=True)
    seg_rows = lax.all_gather(seg_packed, "wide", axis=1, tiled=True)
    count = key_rows.shape[1]
    blocks = count // 32
    stacked = (
        key_rows.reshape(heads_here, blocks, 32, packed_width).transpose(1, 0, 2, 3),
        value_rows.reshape(heads_here, blocks, 32, packed_width).transpose(1, 0, 2, 3),
        seg_rows.reshape(blocks, 512),
    )

    def step_block(state, item):
        return (key_block(state, item[0], item[1], item[2]), None)

    carry, unused = lax.scan(step_block, carry, stacked)
    best, total, accum = carry
    attn = (
        (accum / total[..., None])
        .transpose(1, 0, 2)
        .reshape(tok_rows, local_width)
        .astype(jnp.bfloat16)
    )
    partial_mix = jnp.dot(attn, gathered_out, preferred_element_type=jnp.float32)
    summed_mix = lax.psum_scatter(
        partial_mix.astype(jnp.bfloat16), "narrow", scatter_dimension=0, tiled=True
    ).astype(jnp.float32)
    hidden_out = (hidden_in.astype(jnp.float32) + summed_mix).astype(jnp.bfloat16)
    whole_rows = lax.all_gather(hidden_out, "narrow", axis=0, tiled=True)
    my_columns = lax.dynamic_slice_in_dim(
        whole_rows, lax.axis_index("narrow") * local_width, local_width, 1
    )
    merged_rows = tok_rows // 4
    grouped = my_columns.reshape(merged_rows, 4, local_width)
    partial_feat = jnp.einsum(
        "gjc,jco->go", grouped, gathered_merge, preferred_element_type=jnp.float32
    )
    feature = lax.psum_scatter(
        partial_feat.astype(jnp.bfloat16), "narrow", scatter_dimension=1, tiled=True
    )
    owner_count = lax.axis_size("wide")
    capacity = 2 * merged_rows // owner_count
    owner_col = owners[:, 0]
    onehot = (owner_col[:, None] == jnp.arange(owner_count, dtype=jnp.int32)[None, :]).astype(
        jnp.int32
    )
    rank = jnp.sum(jnp.cumsum(onehot, axis=0) * onehot, axis=1) - 1
    slot = owner_col * capacity + rank
    picker = (jnp.arange(owner_count * capacity, dtype=jnp.int32)[:, None] == slot[None, :]).astype(
        jnp.bfloat16
    )
    outgoing = jnp.dot(picker, feature, preferred_element_type=jnp.float32).astype(jnp.bfloat16)
    outgoing = outgoing.reshape(owner_count, capacity, feature.shape[1])
    arrived = lax.all_to_all(outgoing, "wide", split_axis=0, concat_axis=0, tiled=True)
    return (hidden_out, arrived.reshape(owner_count * capacity, feature.shape[1]))


def solution(mesh):
    return jax.shard_map(
        shards,
        mesh=mesh,
        in_specs=(
            P(("wide", "narrow"), None),
            P("narrow", "wide", None),
            P("narrow", "wide", None),
            P("narrow", "wide", None),
            P("narrow", "wide"),
            P(None, "narrow", "wide"),
            P("wide"),
            P("wide", None),
        ),
        out_specs=(P(("wide", "narrow"), None), P("wide", "narrow")),
        check_vma=False,
    )
```

profile of v0, /device:TPU:32, one launch (start us, length us, event | category | flops | bytes accessed | tf_op | source)
XLA Modules:
  0.0 576.4 jit_solution(16896971549550113275)
XLA Ops:
  9.7 51.9 %all_gather.18 = s32[1,1024,16]{2,0,1:T(1,128)S(1)} all-gather(s32[1,32,16]{2,0,1:T(1,128)S(1)} %copy.25), channel_id=1, replica_groups=mesh['wide'=32,'narrow'=8] {'wide'}, dimensions={1}, use_global_device_ids=true | all-gather | bytes 67584 | tf_op jit(solution)/shard_map/all_gather | solution.py:54
  62.1 2.0 reduce.3
  65.1 49.1 %all-gather = bf16[32,52,208]{2,1,0:T(8,128)(2,1)S(1)} all-gather(bf16[1,52,208]{2,1,0:T(8,128)(2,1)S(1)} %bitcast.77), channel_id=1, replica_groups=mesh['wide'=32,'narrow'=8] {'wide'}, dimensions={0}, use_global_device_ids=true | all-gather | bytes 713856 | tf_op jit(solution)/shard_map/all_gather | solution.py:19
  114.2 1.3 reshape.93
  115.5 82.9 %all-gather.8.cloned.1.call-done = bf16[2,1024,1664]{2,1,0:T(8,128)(2,1)} async-done(((bf16[2,32,1664]{2,1,0:T(8,128)(2,1)}), bf16[2,1024,1664]{2,1,0:T(8,128)(2,1)}) %all-gather.8.cloned.1.call-update) | async-done | bytes 6815760 | tf_op jit(solution)/shard_map/all_gather | solution.py:53
  198.4 167.4 %while.15 = (s32[]{:T(128)}, f32[2,512]{1,0:T(2,128)S(1)}, f32[2,512]{1,0:T(2,128)S(1)}, f32[2,512,104]{1,2,0:T(8,128)S(1)}, s32[32,512]{1,0:T(8,128)S(1)}, /*in...) while((s32[]{:T(128)}, f32[2,512]{1,0:T(2,128)S(1)}, ...), condition=%wide.region_3.4_spmd.clone, body=%wide.region_0.3_spmd.clone.sunk | while | flops 225506304 | bytes 10615425 | solution.py:66
  199.5 1.1 dynamic-slice_bitcast_fusion.3
  204.7 1.1 dynamic-slice_bitcast_fusion.3
  209.9 1.1 dynamic-slice_bitcast_fusion.3
  215.2 1.1 dynamic-slice_bitcast_fusion.3
  220.4 1.1 dynamic-slice_bitcast_fusion.3
  225.6 1.1 dynamic-slice_bitcast_fusion.3
  230.9 1.1 dynamic-slice_bitcast_fusion.3
  236.1 1.1 dynamic-slice_bitcast_fusion.3
  241.3 1.1 dynamic-slice_bitcast_fusion.3
  246.6 1.1 dynamic-slice_bitcast_fusion.3
  251.8 1.1 dynamic-slice_bitcast_fusion.3
  257.0 1.1 dynamic-slice_bitcast_fusion.3
  262.3 1.1 dynamic-slice_bitcast_fusion.3
  267.5 1.1 dynamic-slice_bitcast_fusion.3
  272.7 1.1 dynamic-slice_bitcast_fusion.3
  278.0 1.1 dynamic-slice_bitcast_fusion.3
  283.2 1.1 dynamic-slice_bitcast_fusion.3
  288.4 1.1 dynamic-slice_bitcast_fusion.3
  293.7 1.1 dynamic-slice_bitcast_fusion.3
  298.9 1.1 dynamic-slice_bitcast_fusion.3
  304.1 1.1 dynamic-slice_bitcast_fusion.3
  309.4 1.1 dynamic-slice_bitcast_fusion.3
  314.6 1.1 dynamic-slice_bitcast_fusion.3
  319.8 1.1 dynamic-slice_bitcast_fusion.3
  325.1 1.1 dynamic-slice_bitcast_fusion.3
  330.3 1.1 dynamic-slice_bitcast_fusion.3
  335.5 1.1 dynamic-slice_bitcast_fusion.3
  340.7 1.1 dynamic-slice_bitcast_fusion.3
  346.0 1.1 dynamic-slice_bitcast_fusion.3
  351.2 1.1 dynamic-slice_bitcast_fusion.3
  356.4 1.1 dynamic-slice_bitcast_fusion.3
  361.7 1.1 dynamic-slice_bitcast_fusion.3
  365.9 3.1 convolution_convert_fusion
  369.0 33.3 %reduce-scatter.5.cloned.1.call-done = bf16[64,1664]{1,0:T(8,128)(2,1)} async-done(((bf16[512,1664]{1,0:T(8,128)(2,1)}), bf16[64,1664]{1,0:T(8,128)(2,1)}) %reduce-scatter.5.cloned.1.call-update) | async-done | bytes 213008 | tf_op jit(solution)/shard_map/reduce_scatter | solution.py:75
  402.4 1.7 add_convert_fusion
  404.7 26.0 %all-gather.10.cloned.1.call-done = bf16[512,1664]{1,0:T(8,128)(2,1)} async-done(((bf16[64,1664]{1,0:T(8,128)(2,1)}), bf16[512,1664]{1,0:T(8,128)(2,1)}) %all-gather.10.cloned.1.call-update) | async-done | bytes 1703952 | tf_op jit(solution)/shard_map/all_gather | solution.py:79
  430.8 1.1 constant_dynamic-slice_fusion.1
  432.0 81.6 %all-gather.12.cloned.1.call-done = bf16[4,208,1664]{1,0,2:T(4,128)(2,1)} async-done(((bf16[4,208,52]{1,0,2:T(4,128)(2,1)}), bf16[4,208,1664]{1,0,2:T(4,128)(2,1)}) %all-gather.12.cloned.1.call-update) | async-done | bytes 2768912 | tf_op jit(solution)/shard_map/all_gather | solution.py:20
  513.6 3.8 fusion.23
  517.9 30.2 %reduce-scatter.7.cloned.1.call-done = bf16[208,128]{1,0:T(8,128)(2,1)} async-done(((bf16[1664,128]{1,0:T(8,128)(2,1)}), bf16[208,128]{1,0:T(8,128)(2,1)}) %reduce-scatter.7.cloned.1.call-update) | async-done | bytes 53264
  548.1 1.0 convolution_convert_fusion.1
  549.2 19.6 %all_to_all.5 = bf16[32,8,208]{2,1,0:T(8,128)(2,1)S(1)} all-to-all(bf16[32,8,208]{2,1,0:T(8,128)(2,1)S(1)} %bitcast.71), channel_id=1, replica_groups=mesh['wide'=32,'narrow'=8] {'wide'}, dimensions={0} | all-to-all | bytes 212992 | tf_op jit(solution)/shard_map/all_to_all | solution.py:104
  (424 shorter events, 136.0 us)
Async XLA Ops:
  7.2 57.2 %copy-start.1 = (bf16[2,32,1664]{2,1,0:T(8,128)(2,1)S(1)}, bf16[2,32,1664]{2,1,0:T(8,128)(2,1)}, u32[]{:S(2)}) copy-start(bf16[2,32,1664]{2,1,0:T(8,128)(2,1)} %param.11) | copy-start | bytes 638980
  7.2 57.9 %copy-start.2 = (bf16[208,52]{0,1:T(8,128)(2,1)S(1)}, bf16[208,52]{0,1:T(8,128)(2,1)}, u32[]{:S(2)}) copy-start(bf16[208,52]{0,1:T(8,128)(2,1)} %param.14) | copy-start | bytes 64900
  7.2 108.3 %all-gather.6.cloned.1.call-start = ((), (), s32[]{:S(2)}) async-start(), calls=%async_computation.3 | async-start | bytes 7028736 | tf_op jit(solution)/shard_map/all_gather | solution.py:52
  7.9 190.5 %all-gather.8.cloned.1.call-start = ((), (), s32[]{:S(2)}) async-start(), calls=%async_computation.4 | async-start | bytes 7028736 | tf_op jit(solution)/shard_map/all_gather | solution.py:53
  8.7 393.7 %reduce-scatter.5.cloned.1.call-start = ((), (), s32[]{:S(2)}) async-start(), calls=%async_computation.5 | async-start | bytes 1916928 | tf_op jit(solution)/shard_map/reduce_scatter | solution.py:75
  365.9 36.5 %copy-start = (bf16[64,1664]{1,0:T(8,128)(2,1)S(1)}, bf16[64,1664]{1,0:T(8,128)(2,1)}, u32[]{:S(2)}) copy-start(bf16[64,1664]{1,0:T(8,128)(2,1)} %param.10) | copy-start | bytes 638980
  369.0 61.8 %all-gather.10.cloned.1.call-start = ((), (), s32[]{:S(2)}) async-start(), calls=%async_computation.6 | async-start | bytes 1916928 | tf_op jit(solution)/shard_map/all_gather | solution.py:79
  404.1 109.6 %all-gather.12.cloned.1.call-start = ((), (), s32[]{:S(2)}) async-start(), calls=%async_computation.7 | async-start | bytes 3514368 | tf_op jit(solution)/shard_map/all_gather | solution.py:20
  404.7 143.5 %reduce-scatter.7.cloned.1.call-start = ((), (), s32[]{:S(2)}) async-start(), calls=%async_computation.8 | async-start | bytes 479232
  432.0 85.4 %copy-start.3 = (s32[128,1]{0,1:T(1,128)S(1)}, s32[128,1]{0,1:T(1,128)}, u32[]{:S(2)}) copy-start(s32[128,1]{0,1:T(1,128)} %param.17) | copy-start | bytes 1540
Sparse Core Ops, SparseCore 0:
  10.6 96.3 all-gather.5
  109.6 88.7 all-gather.7
  369.1 33.2 reduce-scatter.4
  404.8 25.9 all-gather.9
  433.5 80.0 all-gather.11
  517.5 30.5 reduce-scatter.6
where the time goes:
time: 578 us; the launch traced here: 576 us
  waiting for transfers between devices  256 us (44%)
  blocking collectives  121 us (21%)
  local copies, waits for them, and re-layouts  101 us (17%)
  matrix products  50.9 us (9%)
  other arithmetic  30.1 us (5%)
  between operations  14.3 us (2%)
    all_gather x1, waiting for transfers between devices, shards(): value_rows = lax.all_gather(values, 'wide', axis=1, tiled=True)  82.9 us
    all_gather x1, waiting for transfers between devices, shards(): lax.all_gather(merge_weight, 'wide', axis=2, tiled=True)  81.6 us
    all_gather x1, blocking collectives, shards(): seg_rows = lax.all_gather(seg_packed, 'wide', axis=1, tiled=True)  51.9 us
    all_gather x1, blocking collectives, shards(): lax.all_gather(out_weight, 'wide', axis=1, tiled=True)  49.1 us
    dynamic_slice x64, local copies, waits for them, and re-layouts, shards(): carry, unused = lax.scan(step_block, carry, stacked)  34.9 us
    reduce_scatter x1, waiting for transfers between devices, shards(): lax.psum_scatter(partial_mix.astype(jnp.bfloat16), 'narrow', scatter_dime...  33.3 us
    unnamed x7, waiting for transfers between devices  32.2 us
    all_gather x1, waiting for transfers between devices, shards(): whole_rows = lax.all_gather(hidden_out, 'narrow', axis=0, tiled=True)  26 us
  transfers between devices with their start and end apart: 6, of which 5 were waited for; matrix products, arithmetic and copies ran while one was open for 1% of the time, Pallas kernels for 0%

commit v1 on v0

--- a/solution.py
+++ b/solution.py
@@ -17,7 +17,9 @@
     seg_packed = tok_seg.reshape(1, packed_rows, 16)
     gathered_out, gathered_merge = (
         lax.all_gather(out_weight, "wide", axis=1, tiled=True),
-        lax.all_gather(merge_weight, "wide", axis=2, tiled=True),
+        jnp.concatenate(
+            lax.all_to_all(jnp.stack([merge_weight] * lax.axis_size("wide")), "wide", 0, 0), axis=2
+        ),
     )
     query_heads = queries.reshape(heads_here, tok_rows, HEAD_DIM)
 

time: 578 us -> 521 us (0.901)
  waiting for transfers between devices: 256 us -> 189 us
  starting transfers between devices: 0.24 us -> 6.69 us
    all_gather x1 -> x0, waiting for transfers between devices: 81.6 us -> none  [shards(): lax.all_gather(merge_weight, 'wide', axis=2, tiled=True)]
    all_to_all x0 -> x1, waiting for transfers between devices: none -> 18.5 us  [shards(): lax.all_to_all(jnp.stack([merge_weight] * lax.axis_size('wide')), 'wide',...]
    reduce_scatter x1, waiting for transfers between devices: 33.3 us -> 24.7 us  [shards(): lax.psum_scatter(partial_mix.astype(jnp.bfloat16), 'narrow', scatter_dime...]
    all_to_all x0 -> x1, starting transfers between devices: none -> 6.49 us  [shards(): lax.all_to_all(jnp.stack([merge_weight] * lax.axis_size('wide')), 'wide',...]
    unnamed x7 -> x6, waiting for transfers between devices: 32.2 us -> 35.8 us
  transfers between devices with their start and end apart: 6 -> 6, of which waited for: 5 -> 5; matrix products, arithmetic and copies ran while one was open for 1% -> 3% of each run, Pallas kernels for 0% -> 0%
where the time goes in v1:
time: 521 us; the launch traced here: 519 us
  waiting for transfers between devices  189 us (36%)
  blocking collectives  121 us (23%)
  local copies, waits for them, and re-layouts  106 us (20%)
  matrix products  49.8 us (10%)
  other arithmetic  30.2 us (6%)
  between operations  13.9 us (3%)
  starting transfers between devices  6.69 us (1%)
    all_gather x1, waiting for transfers between devices, shards(): value_rows = lax.all_gather(values, 'wide', axis=1, tiled=True)  82.9 us
    all_gather x1, blocking collectives, shards(): seg_rows = lax.all_gather(seg_packed, 'wide', axis=1, tiled=True)  51.9 us
    all_gather x1, blocking collectives, shards(): lax.all_gather(out_weight, 'wide', axis=1, tiled=True)  49.1 us
    unnamed x6, waiting for transfers between devices  35.8 us
    dynamic_slice x64, local copies, waits for them, and re-layouts, shards(): carry, unused = lax.scan(step_block, carry, stacked)  34.9 us
    all_gather x1, waiting for transfers between devices, shards(): whole_rows = lax.all_gather(hidden_out, 'narrow', axis=0, tiled=True)  26.8 us
    dot_general x32, matrix products, key_block(): jnp.einsum('hqk,hkd->hqd', weights.astype(jnp.bfloat16), value_heads, pre...  25.8 us
    reduce_scatter x1, waiting for transfers between devices, shards(): lax.psum_scatter(partial_mix.astype(jnp.bfloat16), 'narrow', scatter_dime...  24.7 us
  transfers between devices with their start and end apart: 6, of which 5 were waited for; matrix products, arithmetic and copies ran while one was open for 3% of the time, Pallas kernels for 0%

profile of v1, /device:TPU:32, one launch (start us, length us, event | category | flops | bytes accessed | tf_op | source)
XLA Modules:
  0.0 519.1 jit_solution(10401100013935456285)
XLA Ops:
  9.7 51.9 %all_gather.15 = s32[1,1024,16]{2,0,1:T(1,128)S(1)} all-gather(s32[1,32,16]{2,0,1:T(1,128)S(1)} %copy.26), channel_id=1, replica_groups=mesh['wide'=32,'narrow'=8] {'wide'}, dimensions={1}, use_global_device_ids=true | all-gather | bytes 67584 | tf_op jit(solution)/shard_map/all_gather | solution.py:56
  62.1 2.0 reduce.3
  65.1 49.1 %all-gather = bf16[32,52,208]{2,1,0:T(8,128)(2,1)S(1)} all-gather(bf16[1,52,208]{2,1,0:T(8,128)(2,1)S(1)} %bitcast.81), channel_id=1, replica_groups=mesh['wide'=32,'narrow'=8] {'wide'}, dimensions={0}, use_global_device_ids=true | all-gather | bytes 713856 | tf_op jit(solution)/shard_map/all_gather | solution.py:19
  114.2 1.3 reshape.103
  115.5 82.9 %all-gather.7.cloned.1.call-done = bf16[2,1024,1664]{2,1,0:T(8,128)(2,1)} async-done(((bf16[2,32,1664]{2,1,0:T(8,128)(2,1)}), bf16[2,1024,1664]{2,1,0:T(8,128)(2,1)}) %all-gather.7.cloned.1.call-update) | async-done | bytes 6815760 | tf_op jit(solution)/shard_map/all_gather | solution.py:55
  198.4 167.3 %while.15 = (s32[]{:T(128)}, f32[2,512]{1,0:T(2,128)S(1)}, f32[2,512]{1,0:T(2,128)S(1)}, f32[2,512,104]{1,2,0:T(8,128)S(1)}, s32[32,512]{1,0:T(8,128)S(1)}, /*in...) while((s32[]{:T(128)}, f32[2,512]{1,0:T(2,128)S(1)}, ...), condition=%wide.region_3.4_spmd.clone, body=%wide.region_0.3_spmd.clone.sunk | while | flops 225506304 | bytes 10615425 | solution.py:68
  199.5 1.1 dynamic-slice_bitcast_fusion.3
  204.7 1.1 dynamic-slice_bitcast_fusion.3
  209.9 1.1 dynamic-slice_bitcast_fusion.3
  215.1 1.1 dynamic-slice_bitcast_fusion.3
  220.4 1.1 dynamic-slice_bitcast_fusion.3
  225.6 1.1 dynamic-slice_bitcast_fusion.3
  230.8 1.1 dynamic-slice_bitcast_fusion.3
  236.1 1.1 dynamic-slice_bitcast_fusion.3
  241.3 1.1 dynamic-slice_bitcast_fusion.3
  246.5 1.1 dynamic-slice_bitcast_fusion.3
  251.8 1.1 dynamic-slice_bitcast_fusion.3
  257.0 1.1 dynamic-slice_bitcast_fusion.3
  262.2 1.1 dynamic-slice_bitcast_fusion.3
  267.4 1.1 dynamic-slice_bitcast_fusion.3
  272.7 1.1 dynamic-slice_bitcast_fusion.3
  277.9 1.1 dynamic-slice_bitcast_fusion.3
  283.1 1.1 dynamic-slice_bitcast_fusion.3
  288.4 1.1 dynamic-slice_bitcast_fusion.3
  293.6 1.1 dynamic-slice_bitcast_fusion.3
  298.8 1.1 dynamic-slice_bitcast_fusion.3
  304.1 1.1 dynamic-slice_bitcast_fusion.3
  309.3 1.1 dynamic-slice_bitcast_fusion.3
  314.5 1.1 dynamic-slice_bitcast_fusion.3
  319.7 1.1 dynamic-slice_bitcast_fusion.3
  325.0 1.1 dynamic-slice_bitcast_fusion.3
  330.2 1.1 dynamic-slice_bitcast_fusion.3
  335.4 1.1 dynamic-slice_bitcast_fusion.3
  340.7 1.1 dynamic-slice_bitcast_fusion.3
  345.9 1.1 dynamic-slice_bitcast_fusion.3
  351.1 1.1 dynamic-slice_bitcast_fusion.3
  365.8 3.1 convolution_convert_fusion
  368.9 2.6 stack.2
  371.5 6.5 %all-to-all-start = ((bf16[32,4,208,52]{2,1,3,0:T(4,128)(2,1)}), bf16[32,4,208,52]{2,1,3,0:T(4,128)(2,1)S(1)}, u32[]{:S(2)}, u32[]{:S(2)}) async-start(bf16[32,4,208,52]{2,1,3,0:T(4,128)(2,1)} %stack.2), calls=%async_computation.1 | async-start | bytes 6815744 | tf_op jit(solution)/shard_map/all_to_all | solution.py:21
  378.1 24.7 %reduce-scatter.5.cloned.1.call-done = bf16[64,1664]{1,0:T(8,128)(2,1)} async-done(((bf16[512,1664]{1,0:T(8,128)(2,1)}), bf16[64,1664]{1,0:T(8,128)(2,1)}) %reduce-scatter.5.cloned.1.call-update) | async-done | bytes 213008 | tf_op jit(solution)/shard_map/reduce_scatter | solution.py:77
  402.8 1.8 add_convert_fusion
  404.7 26.8 %all-gather.9.cloned.1.call-done = bf16[512,1664]{1,0:T(8,128)(2,1)} async-done(((bf16[64,1664]{1,0:T(8,128)(2,1)}), bf16[512,1664]{1,0:T(8,128)(2,1)}) %all-gather.9.cloned.1.call-update) | async-done | bytes 1703952 | tf_op jit(solution)/shard_map/all_gather | solution.py:81
  431.5 1.8 constant_dynamic-slice_fusion.1
  433.3 1.7 reshape.97
  435.1 18.5 %all-to-all-done = bf16[32,4,208,52]{2,1,3,0:T(4,128)(2,1)S(1)} async-done(((bf16[32,4,208,52]{2,1,3,0:T(4,128)(2,1)}), bf16[32,4,208,52]{2,1,3,0:T(4,128)(2,1)S(1)}, u32[]{:S(2)}, u32[]{:S(2)}) %all-to-all-start) | async-done | bytes 2768928 | tf_op jit(solution)/shard_map/all_to_all | solution.py:21
  453.6 2.8 fusion.23
  456.8 34.4 %reduce-scatter.7.cloned.1.call-done = bf16[208,128]{1,0:T(8,128)(2,1)} async-done(((bf16[1664,128]{1,0:T(8,128)(2,1)}), bf16[208,128]{1,0:T(8,128)(2,1)}) %reduce-scatter.7.cloned.1.call-update) | async-done | bytes 53264
  492.3 19.5 %all_to_all.10 = bf16[32,8,208]{2,1,0:T(8,128)(2,1)S(1)} all-to-all(bf16[32,8,208]{2,1,0:T(8,128)(2,1)S(1)} %bitcast.75), channel_id=1, replica_groups=mesh['wide'=32,'narrow'=8] {'wide'}, dimensions={0} | all-to-all | bytes 212992 | tf_op jit(solution)/shard_map/all_to_all | solution.py:106
  (424 shorter events, 138.4 us)
Async XLA Ops:
  7.2 57.2 %copy-start = (bf16[2,32,1664]{2,1,0:T(8,128)(2,1)S(1)}, bf16[2,32,1664]{2,1,0:T(8,128)(2,1)}, u32[]{:S(2)}) copy-start(bf16[2,32,1664]{2,1,0:T(8,128)(2,1)} %param.11) | copy-start | bytes 638980
  7.2 57.9 %copy-start.2 = (bf16[208,52]{0,1:T(8,128)(2,1)S(1)}, bf16[208,52]{0,1:T(8,128)(2,1)}, u32[]{:S(2)}) copy-start(bf16[208,52]{0,1:T(8,128)(2,1)} %param.14) | copy-start | bytes 64900
  7.2 108.3 %all-gather.5.cloned.1.call-start = ((), (), s32[]{:S(2)}) async-start(), calls=%async_computation.4 | async-start | bytes 7028736 | tf_op jit(solution)/shard_map/all_gather | solution.py:54
  7.9 190.5 %all-gather.7.cloned.1.call-start = ((), (), s32[]{:S(2)}) async-start(), calls=%async_computation.5 | async-start | bytes 7028736 | tf_op jit(solution)/shard_map/all_gather | solution.py:55
  8.7 394.1 %reduce-scatter.5.cloned.1.call-start = ((), (), s32[]{:S(2)}) async-start(), calls=%async_computation.6 | async-start | bytes 1916928 | tf_op jit(solution)/shard_map/reduce_scatter | solution.py:77
  365.8 3.2 copy-start.1
  371.5 82.0 %all-to-all-start = ((bf16[32,4,208,52]{2,1,3,0:T(4,128)(2,1)}), bf16[32,4,208,52]{2,1,3,0:T(4,128)(2,1)S(1)}, u32[]{:S(2)}, u32[]{:S(2)}) async-start(bf16[32,4,208,52]{2,1,3,0:T(4,128)(2,1)} %stack.2), calls=%async_computation.1 | async-start | bytes 6815744 | tf_op jit(solution)/shard_map/all_to_all | solution.py:21
  378.0 53.5 %all-gather.9.cloned.1.call-start = ((), (), s32[]{:S(2)}) async-start(), calls=%async_computation.7 | async-start | bytes 1916928 | tf_op jit(solution)/shard_map/all_gather | solution.py:81
  404.6 86.6 %reduce-scatter.7.cloned.1.call-start = ((), (), s32[]{:S(2)}) async-start(), calls=%async_computation.8 | async-start | bytes 479232
  453.6 2.8 copy-start.3
Sparse Core Ops, SparseCore 0:
  10.6 96.3 all-gather.4
  109.6 88.6 all-gather.6
  369.0 33.7 reduce-scatter.4
  405.2 26.2 all-gather.8
  456.5 34.6 reduce-scatter.6
